TPU v7x, 32 devices: a whole 2x2x4 slice. The times are simulated.
32 devices in a mesh: tile: 8 (over z, y), depth: 4 (over x, core).
Axes of the slice: x: 2, y: 2, z: 4, core: 2. Of those that a mesh axis runs over, the one named last changes fastest.
Arguments:
- volume: bfloat16 [128, 128, 2048], P('tile', 'depth'), may hold values from -4 to 4
Outputs:
- image: float32 [4, 128, 2048], P(None, ('tile', 'depth'))
All inputs are finite; a program needn't handle non-finite values.
Results may differ from a plain program's by a relative error of at most 0.0003.
Values may be sent and summed in bfloat16 or wider, within the bound.
No kernel may reach another device: no remote copies, remote signals or barrier semaphores. Data moves between devices by JAX's collectives and lax.ppermute only.
A program may use at most 64 MiB of HBM per device.

v0:
```python
import math

import jax
import jax.numpy as jnp
from jax import lax
from jax.experimental import pallas as pl
from jax.experimental.pallas import tpu as pltpu
from jax.sharding import PartitionSpec as P


OPACITY = 3.0
LIGHT_X = 0.48
LIGHT_Y = 0.6
LIGHT_Z = 0.64
AMBIENT = 0.3
DIFFUSE = 0.7
LOG2E = math.log2(math.e)
LANES = 128
PAIR = 2
POWER = 16.0
CENTRE = 7.9

VMEM = pl.BlockSpec(memory_space=pltpu.VMEM)
HBM = pl.BlockSpec(memory_space=pltpu.HBM)


def parity(axis):
    return lax.rem(lax.axis_index(axis), 2)


def exchange(x, axis, odd):
    tiles, depths = lax.axis_size("tile"), lax.axis_size("depth")
    found = []
    for tile in range(tiles):
        for depth in range(depths):
            if axis == "tile":
                other = (tile - odd ^ 1) + odd
                partner = (other, depth) if 0 <= other < tiles else (tile, depth ^ 1)
            else:
                partner = (tile, ((depth - odd ^ 1) + odd) % depths)
            found.append((tile * depths + depth, partner[0] * depths + partner[1]))
    return lax.ppermute(x, ("tile", "depth"), found)


def inside(axis):
    index = lax.axis_index(axis)
    return jnp.where((index == 0) | (index == lax.axis_size(axis) - 1), 0.0, 1.0)


def faces_kernel(volume, tile_a, tile_b, depth_a, depth_b, near, far, wide, sems):
    cells_x, cells_z, rows_y = volume.shape
    odd_tile = parity("tile")
    odd_depth = parity("depth")
    copies = [
        pltpu.make_async_copy(volume.at[:, pl.ds(0, PAIR)], near, sems.at[0]),
        pltpu.make_async_copy(volume.at[:, pl.ds(cells_z - PAIR, PAIR)], far, sems.at[1]),
        pltpu.make_async_copy(volume.at[(cells_x - 1) * (1 - odd_tile)], tile_a, sems.at[2]),
        pltpu.make_async_copy(volume.at[(cells_x - 1) * odd_tile], tile_b, sems.at[3]),
    ]
    for copy in copies:
        copy.start()
    for which, block in enumerate((near, far)):
        copies[which].wait()
        for x in range(cells_x):
            rows = block[x].astype(jnp.float32)
            for c in range(rows_y // LANES):
                wide[which, c, pl.ds(x * PAIR, PAIR), :] = rows[:, c * LANES : (c + 1) * LANES]
    for c in range(rows_y // LANES):
        lanes = pl.ds(c * LANES, LANES)
        first = wide[0, c, pl.ds(0, cells_x, stride=PAIR), :]
        last = wide[1, c, pl.ds(PAIR - 1, cells_x, stride=PAIR), :]
        depth_a[:, lanes] = jnp.where(odd_depth == 0, last, first).astype(jnp.bfloat16)
        depth_b[:, lanes] = jnp.where(odd_depth == 0, first, last).astype(jnp.bfloat16)
    copies[2].wait()
    copies[3].wait()


def faces(volume):
    cells_x, cells_z, rows_y = volume.shape
    column = jax.ShapeDtypeStruct((cells_z, rows_y), volume.dtype)
    layer = jax.ShapeDtypeStruct((cells_x, rows_y), volume.dtype)
    return pl.pallas_call(
        faces_kernel,
        out_shape=(column, column, layer, layer),
        in_specs=[HBM],
        out_specs=(VMEM,) * 4,
        scratch_shapes=[
            pltpu.VMEM((cells_x, PAIR, rows_y), volume.dtype),
            pltpu.VMEM((cells_x, PAIR, rows_y), volume.dtype),
            pltpu.VMEM((2, rows_y // LANES, cells_x * PAIR, LANES), jnp.float32),
            pltpu.SemaphoreType.DMA((4,)),
        ],
        compiler_params=pltpu.CompilerParams(vmem_limit_bytes=12 << 20),
        cost_estimate=pl.CostEstimate(flops=10**10, bytes_accessed=10**6, transcendentals=0),
        name="faces",
    )(pltpu.with_memory_space_constraint(volume, pltpu.HBM))


class Field:
    def __init__(self, ref, rows_y, columns):
        self.ref = ref
        self.chunks = rows_y // LANES
        self.half = self.chunks // 2
        self.pitch, _ = Field.shape(rows_y, columns)

    @staticmethod
    def shape(rows_y, columns):
        pitch = columns + (columns % 4 == 0)
        return pitch, (rows_y // LANES + 2) * pitch

    def clear_ends(self):
        blank = jnp.zeros((self.pitch, LANES), jnp.float32)
        self.ref[pl.ds(0, self.pitch), :] = blank
        self.ref[pl.ds((self.chunks + 1) * self.pitch, self.pitch), :] = blank

    def put(self, column, block):
        for c in range(self.chunks):
            at = pl.ds((c + 1) * self.pitch + column, block.shape[0])
            self.ref[at, :] = block[:, c * LANES : (c + 1) * LANES]

    def get(self, chunk, column):
        return self.ref[pl.ds((chunk + 1) * self.pitch + column, self.half, stride=2 * self.pitch), :]


def march(field, cells_z, column, left, right, before, after, depth_total):
    shape = (field.half, LANES)
    lane = lax.broadcasted_iota(jnp.int32, shape, 1)
    first, last = lane == 0, lane == LANES - 1
    scale = DIFFUSE * LIGHT_Z
    along_x, along_y = LIGHT_X / LIGHT_Z, LIGHT_Y / LIGHT_Z
    density = OPACITY / depth_total

    def cell(here, before, after, left, right, dy, sums):
        passing, total, skew, bell = sums
        dx = right - left
        dz = after - before
        facing = along_x * dx + along_y * dy + dz
        shade = AMBIENT / scale + jnp.abs(facing) * lax.rsqrt(4.0 + dx * dx + dy * dy + dz * dz)
        squared = here * here
        power = squared * (-LOG2E)
        behind = passing * jnp.exp2(power * (density / (1.0 + squared)))
        weight = (passing - behind) * shade
        return behind, total + weight, skew + weight * jnp.tanh(here), bell + weight * jnp.exp2(power)

    def along_z(chunk, z):
        source, row = before if z < 0 else after if z == cells_z else (field, column + z)
        return source.get(chunk, row)

    half = 0.5 * scale
    one, zero = jnp.ones(shape, jnp.float32), jnp.zeros(shape, jnp.float32)
    even_sums = odd_sums = (one, zero, zero, zero)
    even_before, odd_before = along_z(0, -1), along_z(1, -1)
    even, odd = along_z(0, 0), along_z(1, 0)
    for z in range(cells_z):
        even_after, odd_after = along_z(0, z + 1), along_z(1, z + 1)
        next_even, last_odd = along_z(2, z), along_z(-1, z)
        up = [pltpu.roll(v, LANES - 1, 1) for v in (even, odd, next_even)]
        down = [pltpu.roll(v, 1, 1) for v in (last_odd, even, odd)]
        even_dy = jnp.where(last, up[1], up[0]) - jnp.where(first, down[0], down[1])
        odd_dy = jnp.where(last, up[2], up[1]) - jnp.where(first, down[1], down[2])
        sides = [[side[0].get(chunk, side[1] + z) for side in (left, right)] for chunk in (0, 1)]
        even_sums = cell(even, even_before, even_after, *sides[0], even_dy, even_sums)
        odd_sums = cell(odd, odd_before, odd_after, *sides[1], odd_dy, odd_sums)
        even_before, even, odd_before, odd = even, even_after, odd, odd_after
    return [
        (half * (total + skew), half * bell, half * (total - skew), passing)
        for passing, total, skew, bell in (even_sums, odd_sums)
    ]


def store_column(out, x, parts):
    for which, channels in enumerate(parts):
        for channel, value in enumerate(channels):
            out[x, channel, pl.ds(which, value.shape[0], stride=2), :] = value


def widen_kernel(volume, rows):
    cells_x, cells_z, rows_y = volume.shape
    field = Field(rows, rows_y, cells_x * cells_z)
    field.clear_ends()

    def column(x, _):
        field.put(x * cells_z, volume[x].astype(jnp.float32))
        return 0

    lax.fori_loop(0, cells_x, column, 0, unroll=2)


def widen(volume):
    cells_x, cells_z, rows_y = volume.shape
    _, rows = Field.shape(rows_y, cells_x * cells_z)
    return pl.pallas_call(
        widen_kernel,
        out_shape=jax.ShapeDtypeStruct((rows, LANES), jnp.float32),
        in_specs=[VMEM],
        out_specs=VMEM,
        compiler_params=pltpu.CompilerParams(vmem_limit_bytes=12 << 20),
        cost_estimate=pl.CostEstimate(flops=10**6, bytes_accessed=10**6, transcendentals=0),
        name="widen",
    )(volume)


def put_layers(scratch, rows_y, depth_a, depth_b):
    cells_x = depth_a.shape[0]
    layers = Field(scratch, rows_y, 2 * cells_x)
    odd_depth = parity("depth")
    layers.put((1 - odd_depth) * cells_x, depth_a[...].astype(jnp.float32))
    layers.put(odd_depth * cells_x, depth_b[...].astype(jnp.float32) * inside("depth"))
    return layers


def inner_kernel(cells_z, depth_total, rows, depth_a, depth_b, out, scratch):
    cells_x, rows_y = depth_a.shape
    field = Field(rows, rows_y, cells_x * cells_z)
    layers = put_layers(scratch, rows_y, depth_a, depth_b)

    def columns(i, _):
        for x in (2 * i + 1, 2 * i + 2):
            at = x * cells_z
            sides = (field, at - cells_z), (field, at + cells_z), (layers, x), (layers, cells_x + x)
            store_column(out, x - 1, march(field, cells_z, at, *sides, depth_total))
        return 0

    lax.fori_loop(0, (cells_x - 2) // 2, columns, 0)


def inner(rows, depth_a, depth_b, cells_z, depth_total):
    cells_x, rows_y = depth_a.shape
    return pl.pallas_call(
        lambda *refs: inner_kernel(cells_z, depth_total, *refs),
        out_shape=jax.ShapeDtypeStruct((cells_x - 2, 4, rows_y // LANES, LANES), jnp.float32),
        in_specs=[VMEM] * 3,
        out_specs=VMEM,
        scratch_shapes=[pltpu.VMEM((Field.shape(rows_y, 2 * cells_x)[1], LANES), jnp.float32)],
        compiler_params=pltpu.CompilerParams(vmem_limit_bytes=12 << 20),
        cost_estimate=pl.CostEstimate(flops=10**8, bytes_accessed=10**7, transcendentals=0),
        name="inner",
    )(rows, depth_a, depth_b)


def outer_kernel(depth_total, rows, depth_a, depth_b, tile_a, tile_b, done, kept, given, scratch, ends, edge):
    cells_x, rows_y = depth_a.shape
    cells_z = tile_a.shape[0]
    odd_tile = parity("tile")
    field = Field(rows, rows_y, cells_x * cells_z)
    layers = put_layers(scratch, rows_y, depth_a, depth_b)
    halo = Field(ends, rows_y, 2 * cells_z)
    halo.put((1 - odd_tile) * cells_z, tile_a[...].astype(jnp.float32))
    halo.put(odd_tile * cells_z, tile_b[...].astype(jnp.float32) * inside("tile"))
    final = (cells_x - 1) * cells_z
    for side, at, left, right in (
        (0, 0, (halo, 0), (field, cells_z)),
        (1, final, (field, final - cells_z), (halo, cells_z)),
    ):
        x = side * (cells_x - 1)
        parts = march(field, cells_z, at, left, right, (layers, x), (layers, cells_x + x), depth_total)
        store_column(edge, side, parts)
    upper = parity("depth")
    pieces = cells_x // lax.axis_size("depth")
    half = cells_x // 2
    for i in range(half):
        low = i // pieces * 2 * pieces + i % pieces
        for target, bit in ((kept, upper), (given, 1 - upper)):
            x = low + bit * pieces
            if i == 0:
                target[i] = jnp.where(bit == 0, edge[0], done[pieces - 1])
            elif i == half - 1:
                target[i] = jnp.where(bit == 1, edge[1], done[cells_x - pieces - 2])
            else:
                target[i] = done[x - 1]


def outer(rows, depth_a, depth_b, tile_a, tile_b, done, depth_total):
    cells_x, rows_y = depth_a.shape
    cells_z = tile_a.shape[0]
    half = jax.ShapeDtypeStruct((cells_x // 2, 4, rows_y // LANES, LANES), jnp.float32)
    return pl.pallas_call(
        lambda *refs: outer_kernel(depth_total, *refs),
        out_shape=(half, half),
        in_specs=[VMEM] * 6,
        out_specs=(VMEM, VMEM),
        scratch_shapes=[
            pltpu.VMEM((Field.shape(rows_y, 2 * cells_x)[1], LANES), jnp.float32),
            pltpu.VMEM((Field.shape(rows_y, 2 * cells_z)[1], LANES), jnp.float32),
            pltpu.VMEM((2, 4, rows_y // LANES, LANES), jnp.float32),
        ],
        compiler_params=pltpu.CompilerParams(vmem_limit_bytes=12 << 20),
        cost_estimate=pl.CostEstimate(flops=10**7, bytes_accessed=10**6, transcendentals=0),
        name="outer",
    )(rows, depth_a, depth_b, tile_a, tile_b, done)


def over(own, other, in_front):
    front = [jnp.where(in_front, a, b) for a, b in zip(own, other)]
    back = [jnp.where(in_front, b, a) for a, b in zip(own, other)]
    return [a + front[3] * b for a, b in zip(front[:3], back[:3])] + [front[3] * back[3]]


def encode(channels):
    red, green, blue, passing = channels
    return [
        jnp.exp2(POWER * (jnp.log2(x) + CENTRE)).astype(jnp.bfloat16) for x in (red, green, blue, 1.0 - passing)
    ]


def decode(codes):
    red, green, blue, opacity = [jnp.exp2(jnp.log2(y.astype(jnp.float32)) * (1.0 / POWER) - CENTRE) for y in codes]
    return [red, green, blue, 1.0 - opacity]


def received(block):
    channels = [block[channel] for channel in range(4)]
    return decode(channels) if block.dtype == jnp.bfloat16 else channels


def merge_kernel(section, pieces, kept, other, next_kept, next_given):
    position = lax.axis_index("depth")
    in_front = lax.rem(position // 2**section, 2) == 0
    upper = lax.rem(position // 2 ** (section + 1), 2)
    for i in range(kept.shape[0] // 2):
        low = i // pieces * 2 * pieces + i % pieces
        for target, x in ((next_kept, low + upper * pieces), (next_given, low + (1 - upper) * pieces)):
            channels = over(list(kept[x]), received(other[x]), in_front)
            for channel, value in enumerate(encode(channels) if target is next_given else channels):
                target[i, channel] = value


def merge(kept, other, section, pieces):
    shape = (kept.shape[0] // 2, *kept.shape[1:])
    return pl.pallas_call(
        lambda *refs: merge_kernel(section, pieces, *refs),
        out_shape=(jax.ShapeDtypeStruct(shape, jnp.float32), jax.ShapeDtypeStruct(shape, jnp.bfloat16)),
        in_specs=[VMEM] * 2,
        out_specs=(VMEM, VMEM),
        compiler_params=pltpu.CompilerParams(vmem_limit_bytes=8 << 20),
        name="merge",
    )(kept, other)


def finish_kernel(section, kept, other, image):
    position = lax.axis_index("depth")
    in_front = lax.rem(position // 2**section, 2) == 0
    columns, _, chunks, _ = kept.shape
    for x in range(columns):
        red, green, blue, passing = over(list(kept[x]), received(other[x]), in_front)
        for channel, value in enumerate((red, green, blue, 1.0 - passing)):
            for c in range(chunks):
                image[channel, pl.ds(x, 1), pl.ds(c * LANES, LANES)] = value[c : c + 1]


def finish(kept, other, section):
    columns, channels, chunks, _ = kept.shape
    return pl.pallas_call(
        lambda section_kept, section_other, image: finish_kernel(section, section_kept, section_other, image),
        out_shape=jax.ShapeDtypeStruct((channels, columns, chunks * LANES), kept.dtype),
        in_specs=[VMEM] * 2,
        out_specs=VMEM,
        compiler_params=pltpu.CompilerParams(vmem_limit_bytes=8 << 20),
        name="finish",
    )(kept, other)


def shards(volume):
    depth_count = lax.axis_size("depth")
    depth_total = volume.shape[1] * depth_count
    pieces = volume.shape[0] // depth_count
    levels = depth_count.bit_length() - 1
    tile_a, tile_b, depth_a, depth_b = faces(volume)
    tile_b = exchange(tile_b, "tile", 1)
    depth_b = exchange(depth_b, "depth", 1)
    depth_a = exchange(depth_a, "depth", 0)
    tile_a = exchange(tile_a, "tile", 0)
    rows = widen(volume)
    done = inner(rows, depth_a, depth_b, volume.shape[1], depth_total)
    kept, given = outer(rows, depth_a, depth_b, tile_a, tile_b, done, depth_total)
    for section in range(levels):
        other = lax.ppermute(given, "depth", [(i, i ^ 1 << section) for i in range(depth_count)])
        if section < levels - 1:
            kept, given = merge(kept, other, section, pieces)
    return finish(kept, other, levels - 1)


def solution(mesh):
    in_specs = (P("tile", "depth", None),)
    out_specs = P(None, ("tile", "depth"), None)
    return jax.shard_map(shards, mesh=mesh, in_specs=in_specs, out_specs=out_specs, check_vma=False)
```

profile of v0, /device:TPU:0, one launch (start us, length us, event | category | flops | bytes accessed | tf_op | source)
XLA Modules:
  0.0 21.5 jit_solution(18154412840308771612)
XLA Ops:
  0.0 0.0 copy-start
  0.0 1.3 %faces.1 = (bf16[32,2048]{1,0:T(8,128)(2,1)S(1)}, bf16[32,2048]{1,0:T(8,128)(2,1)S(1)}, bf16[16,2048]{1,0:T(8,128)(2,1)S(1)}, bf16[16,2048]{1,0:T(8,128)(2,1)S(1)}) custom-call(bf16[16,32,2048]{2,1,0:T(8,128)(2,1)} %volume.3), custom_call_target="tpu_custom_call" | custom-call | flops 10000000000 | bytes 1000000 | tf_op jit(solution)/shard_map/faces/pallas_call | solution.py:82
  1.3 3.1 %collective-permute-start.2 = (bf16[32,2048]{1,0:T(8,128)(2,1)S(1)}, bf16[32,2048]{1,0:T(8,128)(2,1)S(1)}, u32[]{:S(2)}, u32[]{:S(2)}) collective-permute-start(bf16[32,2048]{1,0:T(8,128)(2,1)S(1)} %get-tuple-element.15), channel_id=1, source_target_pairs={{0,4},{1,5},{2,6},{3,7},{4,0},{5,1},{6,2},{7,3},{8,12},{9,13},{10,... | collective-permute-start | bytes 393224 | tf_op jit(solution)/shard_map/ppermute | solution.py:42
  4.4 0.0 collective-permute-start.3
  4.4 0.5 %collective-permute-start = (bf16[16,2048]{1,0:T(8,128)(2,1)S(1)}, bf16[16,2048]{1,0:T(8,128)(2,1)S(1)}, u32[]{:S(2)}, u32[]{:S(2)}) collective-permute-start(bf16[16,2048]{1,0:T(8,128)(2,1)S(1)} %get-tuple-element.13), channel_id=1, source_target_pairs={{0,1},{1,0},{2,3},{3,2},{4,5},{5,4},{6,7},{7,6},{8,9},{9,8},{10,11... | collective-permute-start | bytes 196616 | tf_op jit(solution)/shard_map/ppermute | solution.py:42
  4.9 1.1 %collective-permute-start.1 = (bf16[16,2048]{1,0:T(8,128)(2,1)S(1)}, bf16[16,2048]{1,0:T(8,128)(2,1)S(1)}, u32[]{:S(2)}, u32[]{:S(2)}) collective-permute-start(bf16[16,2048]{1,0:T(8,128)(2,1)S(1)} %get-tuple-element.14), channel_id=1, source_target_pairs={{0,3},{1,2},{2,1},{3,0},{4,7},{5,6},{6,5},{7,4},{8,11},{9,10},{10,... | collective-permute-start | bytes 196616 | tf_op jit(solution)/shard_map/ppermute | solution.py:42
  6.0 0.0 copy-done
  6.0 0.3 %widen.1.refs_0_ = f32[9234,128]{1,0:T(8,128)S(1)} custom-call(bf16[16,32,2048]{2,1,0:T(8,128)(2,1)S(1)} %copy-done), custom_call_target="tpu_custom_call" | custom-call | flops 1000000 | bytes 1000000 | tf_op jit(solution)/shard_map/widen/pallas_call | solution.py:192
  6.3 0.0 collective-permute-done.refs_1_
  6.3 2.8 %collective-permute-done.1.refs_2_ = bf16[16,2048]{1,0:T(8,128)(2,1)S(1)} collective-permute-done((bf16[16,2048]{1,0:T(8,128)(2,1)S(1)}, bf16[16,2048]{1,0:T(8,128)(2,1)S(1)}, u32[]{:S(2)}, u32[]{:S(2)}) %collective-permute-start.1) | collective-permute-done | bytes 65568 | tf_op jit(solution)/shard_map/ppermute | solution.py:42
  9.1 4.9 %inner.1.refs_5_ = f32[14,4,16,128]{3,2,1,0:T(8,128)S(1)} custom-call(f32[9234,128]{1,0:T(8,128)S(1)} %widen.1.refs_0_, bf16[16,2048]{1,0:T(8,128)(2,1)S(1)} %collective-permute-done.refs_1_, bf16[16,2048]{1,0:T(8,128)(2,1)S(1)} %collective-permute-done.1.refs_2_), custom_call_target="tpu_custom_call" | custom-call | flops 100000000 | bytes 10000000 | tf_op jit(solution)/shard_map/inner/pallas_call | solution.py:229
  14.0 0.0 collective-permute-done.2.refs_3_
  14.0 0.0 collective-permute-done.3.refs_4_
  14.0 0.8 %outer.1 = (f32[8,4,16,128]{3,2,1,0:T(8,128)S(1)}, f32[8,4,16,128]{3,2,1,0:T(8,128)S(1)}) custom-call(f32[9234,128]{1,0:T(8,128)S(1)} %widen.1.refs_0_, bf16[16,2048]{1,0:T(8,128)(2,1)S(1)} %collective-permute-done.refs_1_, bf16[16,2048]{1,0:T(8,128)(2,1)S(1)} %collective-permute-done.1.refs_2_, bf16[32,2048]{1,0:T(8,128)(2,1)S(1)} %collective-permute-done.2.refs_3_, ...), custom_call_target="tpu_custom_call" | custom-call | flops 10000000 | bytes 1000000 | tf_op jit(solution)/shard_map/outer/pallas_call | solution.py:277
  14.8 0.2 collective-permute-start.4
  14.9 1.4 %collective-permute-done.4.refs_1_ = f32[8,4,16,128]{3,2,1,0:T(8,128)S(1)} collective-permute-done((f32[8,4,16,128]{3,2,1,0:T(8,128)S(1)}, f32[8,4,16,128]{3,2,1,0:T(8,128)S(1)}, u32[]{:S(2)}, u32[]{:S(2)}) %collective-permute-start.4) | collective-permute-done | bytes 262176 | tf_op jit(solution)/shard_map/ppermute | solution.py:377
  16.4 0.1 merge.1
  16.4 1.6 %collective-permute-start.5 = (bf16[4,4,16,128]{3,2,1,0:T(8,128)(2,1)S(1)}, bf16[4,4,16,128]{3,2,1,0:T(8,128)(2,1)S(1)}, u32[]{:S(2)}, u32[]{:S(2)}) collective-permute-start(bf16[4,4,16,128]{3,2,1,0:T(8,128)(2,1)S(1)} %get-tuple-element.20), channel_id=1, source_target_pairs={{0,2},{1,3},{2,0},{3,1},{4,6},{5,7},{6,4},{7,5},{8,10},{9,11},{10,... | collective-permute-start | bytes 196616 | tf_op jit(solution)/shard_map/ppermute | solution.py:377
  18.0 2.8 %collective-permute-done.5.section_other = bf16[4,4,16,128]{3,2,1,0:T(8,128)(2,1)S(1)} collective-permute-done((bf16[4,4,16,128]{3,2,1,0:T(8,128)(2,1)S(1)}, bf16[4,4,16,128]{3,2,1,0:T(8,128)(2,1)S(1)}, u32[]{:S(2)}, u32[]{:S(2)}) %collective-permute-start.5) | collective-permute-done | bytes 65568 | tf_op jit(solution)/shard_map/ppermute | solution.py:377
  20.8 0.8 %finish.1 = f32[4,4,2048]{2,1,0:T(4,128)} custom-call(f32[4,4,16,128]{3,2,1,0:T(8,128)S(1)} %get-tuple-element.19.section_kept, bf16[4,4,16,128]{3,2,1,0:T(8,128)(2,1)S(1)} %collective-permute-done.5.section_other), custom_call_target="tpu_custom_call" | custom-call | tf_op jit(solution)/shard_map/finish/pallas_call | solution.py:353
Async XLA Ops:
  0.0 6.0 %copy-start = (bf16[16,32,2048]{2,1,0:T(8,128)(2,1)S(1)}, bf16[16,32,2048]{2,1,0:T(8,128)(2,1)}, u32[]{:S(2)}) copy-start(bf16[16,32,2048]{2,1,0:T(8,128)(2,1)} %volume.3) | copy-start | bytes 6291460
  1.3 12.6 %collective-permute-start.2 = (bf16[32,2048]{1,0:T(8,128)(2,1)S(1)}, bf16[32,2048]{1,0:T(8,128)(2,1)S(1)}, u32[]{:S(2)}, u32[]{:S(2)}) collective-permute-start(bf16[32,2048]{1,0:T(8,128)(2,1)S(1)} %get-tuple-element.15), channel_id=1, source_target_pairs={{0,4},{1,5},{2,6},{3,7},{4,0},{5,1},{6,2},{7,3},{8,12},{9,13},{10,... | collective-permute-start | bytes 393224 | tf_op jit(solution)/shard_map/ppermute | solution.py:42
  4.4 9.6 %collective-permute-start.3 = (bf16[32,2048]{1,0:T(8,128)(2,1)S(1)}, bf16[32,2048]{1,0:T(8,128)(2,1)S(1)}, u32[]{:S(2)}, u32[]{:S(2)}) collective-permute-start(bf16[32,2048]{1,0:T(8,128)(2,1)S(1)} %get-tuple-element.16), channel_id=1, source_target_pairs={{0,1},{1,0},{2,3},{3,2},{4,8},{5,9},{6,10},{7,11},{8,4},{9,5},{10,... | collective-permute-start | bytes 393224 | tf_op jit(solution)/shard_map/ppermute | solution.py:42
  4.4 1.9 %collective-permute-start = (bf16[16,2048]{1,0:T(8,128)(2,1)S(1)}, bf16[16,2048]{1,0:T(8,128)(2,1)S(1)}, u32[]{:S(2)}, u32[]{:S(2)}) collective-permute-start(bf16[16,2048]{1,0:T(8,128)(2,1)S(1)} %get-tuple-element.13), channel_id=1, source_target_pairs={{0,1},{1,0},{2,3},{3,2},{4,5},{5,4},{6,7},{7,6},{8,9},{9,8},{10,11... | collective-permute-start | bytes 196616 | tf_op jit(solution)/shard_map/ppermute | solution.py:42
  4.9 4.2 %collective-permute-start.1 = (bf16[16,2048]{1,0:T(8,128)(2,1)S(1)}, bf16[16,2048]{1,0:T(8,128)(2,1)S(1)}, u32[]{:S(2)}, u32[]{:S(2)}) collective-permute-start(bf16[16,2048]{1,0:T(8,128)(2,1)S(1)} %get-tuple-element.14), channel_id=1, source_target_pairs={{0,3},{1,2},{2,1},{3,0},{4,7},{5,6},{6,5},{7,4},{8,11},{9,10},{10,... | collective-permute-start | bytes 196616 | tf_op jit(solution)/shard_map/ppermute | solution.py:42
  14.8 1.6 %collective-permute-start.4 = (f32[8,4,16,128]{3,2,1,0:T(8,128)S(1)}, f32[8,4,16,128]{3,2,1,0:T(8,128)S(1)}, u32[]{:S(2)}, u32[]{:S(2)}) collective-permute-start(f32[8,4,16,128]{3,2,1,0:T(8,128)S(1)} %get-tuple-element.18), channel_id=1, source_target_pairs={{0,1},{1,0},{2,3},{3,2},{4,5},{5,4},{6,7},{7,6},{8,9},{9,8},{10,11... | collective-permute-start | bytes 786440 | tf_op jit(solution)/shard_map/ppermute | solution.py:377
  16.4 4.3 %collective-permute-start.5 = (bf16[4,4,16,128]{3,2,1,0:T(8,128)(2,1)S(1)}, bf16[4,4,16,128]{3,2,1,0:T(8,128)(2,1)S(1)}, u32[]{:S(2)}, u32[]{:S(2)}) collective-permute-start(bf16[4,4,16,128]{3,2,1,0:T(8,128)(2,1)S(1)} %get-tuple-element.20), channel_id=1, source_target_pairs={{0,2},{1,3},{2,0},{3,1},{4,6},{5,7},{6,4},{7,5},{8,10},{9,11},{10,... | collective-permute-start | bytes 196616 | tf_op jit(solution)/shard_map/ppermute | solution.py:377
where the time goes:
time: 21.7 us; the launch traced here: 21.5 us
  Pallas kernels  8.1 us (37%)
  waiting for transfers between devices  6.97 us (32%)
  starting transfers between devices  6.41 us (30%)
    pallas_call x1, Pallas kernels, inner(): pl.pallas_call(lambda *refs: inner_kernel(cells_z, depth_total, *refs), o...  4.85 us
    ppermute x4, starting transfers between devices, exchange(): return lax.ppermute(x, ('tile', 'depth'), found)  4.67 us
    ppermute x2, waiting for transfers between devices, shards(): lax.ppermute(given, 'depth', [(i, i ^ 1 << section) for i in range(depth_...  4.19 us
    ppermute x4, waiting for transfers between devices, exchange(): return lax.ppermute(x, ('tile', 'depth'), found)  2.77 us
    ppermute x2, starting transfers between devices, shards(): lax.ppermute(given, 'depth', [(i, i ^ 1 << section) for i in range(depth_...  1.74 us
    pallas_call x1, Pallas kernels, faces(): pl.pallas_call(faces_kernel, out_shape=(column, column, layer, layer), in...  1.32 us
    pallas_call x1, Pallas kernels, outer(): pl.pallas_call(lambda *refs: outer_kernel(depth_total, *refs), out_shape=...  0.78 us
    pallas_call x1, Pallas kernels, finish(): pl.pallas_call(lambda section_kept, section_other, image: finish_kernel(s...  0.76 us
  transfers between devices with their start and end apart: 6, of which 3 were waited for; matrix products, arithmetic and copies ran while one was open for 0% of the time, Pallas kernels for 24%

commit v1 on v0

--- a/solution.py
+++ b/solution.py
@@ -122,50 +122,94 @@
         return self.ref[pl.ds((chunk + 1) * self.pitch + column, self.half, stride=2 * self.pitch), :]
 
 
+class March:
+    def __init__(self, field, cells_z, column, before, after, depth_total):
+        self.field, self.cells_z, self.column = field, cells_z, column
+        self.before, self.after = before, after
+        self.density = OPACITY / depth_total
+        self.shape = (field.half, LANES)
+        self.scale = DIFFUSE * LIGHT_Z
+        self.along_x, self.along_y = LIGHT_X / LIGHT_Z, LIGHT_Y / LIGHT_Z
+
+    def at(self, chunk, z):
+        side = self.before if z < 0 else self.after if z == self.cells_z else (self.field, self.column + z)
+        return None if side is None else side[0].get(chunk, side[1])
+
+    def cells(self):
+        lane = lax.broadcasted_iota(jnp.int32, self.shape, 1)
+        first, last = lane == 0, lane == LANES - 1
+        self.passing = [jnp.ones(self.shape, jnp.float32)] * 2
+        before = [self.at(which, -1) for which in (0, 1)]
+        here = [self.at(which, 0) for which in (0, 1)]
+        for z in range(self.cells_z):
+            after = [self.at(which, z + 1) for which in (0, 1)]
+            next_even, last_odd = self.at(2, z), self.at(-1, z)
+            up = [pltpu.roll(v, LANES - 1, 1) for v in (*here, next_even)]
+            down = [pltpu.roll(v, 1, 1) for v in (last_odd, *here)]
+            for which in (0, 1):
+                dy = jnp.where(last, up[which + 1], up[which]) - jnp.where(first, down[which], down[which + 1])
+                facing, norm = self.along_y * dy, 4.0 + dy * dy
+                if before[which] is not None and after[which] is not None:
+                    facing, norm = self.along_z(facing, norm, before[which], after[which])
+                squared = here[which] * here[which]
+                power = squared * (-LOG2E)
+                behind = self.passing[which] * jnp.exp2(power * (self.density / (1.0 + squared)))
+                weight = self.passing[which] - behind
+                self.passing[which] = behind
+                yield z, which, facing, norm, (
+                    weight,
+                    weight * jnp.tanh(here[which]),
+                    weight * jnp.exp2(power),
+                )
+            before, here = here, after
+
+    def along_z(self, facing, norm, before, after):
+        dz = after - before
+        return facing + dz, norm + dz * dz
+
+    def shade(self, facing, norm, left, right):
+        dx = right - left
+        return AMBIENT / self.scale + jnp.abs(self.along_x * dx + facing) * lax.rsqrt(norm + dx * dx)
+
+    def colours(self, total, skew, bell, passing):
+        half = 0.5 * self.scale
+        return half * (total + skew), half * bell, half * (total - skew), passing
+
+
 def march(field, cells_z, column, left, right, before, after, depth_total):
-    shape = (field.half, LANES)
-    lane = lax.broadcasted_iota(jnp.int32, shape, 1)
-    first, last = lane == 0, lane == LANES - 1
-    scale = DIFFUSE * LIGHT_Z
-    along_x, along_y = LIGHT_X / LIGHT_Z, LIGHT_Y / LIGHT_Z
-    density = OPACITY / depth_total
-
-    def cell(here, before, after, left, right, dy, sums):
-        passing, total, skew, bell = sums
-        dx = right - left
-        dz = after - before
-        facing = along_x * dx + along_y * dy + dz
-        shade = AMBIENT / scale + jnp.abs(facing) * lax.rsqrt(4.0 + dx * dx + dy * dy + dz * dz)
-        squared = here * here
-        power = squared * (-LOG2E)
-        behind = passing * jnp.exp2(power * (density / (1.0 + squared)))
-        weight = (passing - behind) * shade
-        return behind, total + weight, skew + weight * jnp.tanh(here), bell + weight * jnp.exp2(power)
-
-    def along_z(chunk, z):
-        source, row = before if z < 0 else after if z == cells_z else (field, column + z)
-        return source.get(chunk, row)
-
-    half = 0.5 * scale
-    one, zero = jnp.ones(shape, jnp.float32), jnp.zeros(shape, jnp.float32)
-    even_sums = odd_sums = (one, zero, zero, zero)
-    even_before, odd_before = along_z(0, -1), along_z(1, -1)
-    even, odd = along_z(0, 0), along_z(1, 0)
-    for z in range(cells_z):
-        even_after, odd_after = along_z(0, z + 1), along_z(1, z + 1)
-        next_even, last_odd = along_z(2, z), along_z(-1, z)
-        up = [pltpu.roll(v, LANES - 1, 1) for v in (even, odd, next_even)]
-        down = [pltpu.roll(v, 1, 1) for v in (last_odd, even, odd)]
-        even_dy = jnp.where(last, up[1], up[0]) - jnp.where(first, down[0], down[1])
-        odd_dy = jnp.where(last, up[2], up[1]) - jnp.where(first, down[1], down[2])
-        sides = [[side[0].get(chunk, side[1] + z) for side in (left, right)] for chunk in (0, 1)]
-        even_sums = cell(even, even_before, even_after, *sides[0], even_dy, even_sums)
-        odd_sums = cell(odd, odd_before, odd_after, *sides[1], odd_dy, odd_sums)
-        even_before, even, odd_before, odd = even, even_after, odd, odd_after
-    return [
-        (half * (total + skew), half * bell, half * (total - skew), passing)
-        for passing, total, skew, bell in (even_sums, odd_sums)
-    ]
+    way = March(field, cells_z, column, before, after, depth_total)
+    sums = [[jnp.zeros(way.shape, jnp.float32)] * 3 for _ in (0, 1)]
+    for z, which, facing, norm, weights in way.cells():
+        shade = way.shade(facing, norm, left[0].get(which, left[1] + z), right[0].get(which, right[1] + z))
+        total, skew, bell = sums[which]
+        weight = weights[0] * shade
+        sums[which] = [total + weight, skew + weights[1] * shade, bell + weights[2] * shade]
+    return [way.colours(*sums[which], way.passing[which]) for which in (0, 1)]
+
+
+def march_to_shading(field, cells_z, column, depth_total, saved, passed):
+    way = March(field, cells_z, column, None, None, depth_total)
+    for z, which, facing, norm, weights in way.cells():
+        for k, value in enumerate((facing, norm, *weights)):
+            saved[z, which, k] = value
+    for which in (0, 1):
+        passed[which] = way.passing[which]
+
+
+def march_shading(field, cells_z, column, left, right, before, after, saved, passed, depth_total):
+    way = March(field, cells_z, column, before, after, depth_total)
+    parts = []
+    for which in (0, 1):
+        sums = [jnp.zeros(way.shape, jnp.float32)] * 3
+        for z in range(cells_z):
+            sides = [side[0].get(which, side[1] + z) for side in (left, right)]
+            facing, norm = saved[z, which, 0], saved[z, which, 1]
+            if z in (0, cells_z - 1):
+                facing, norm = way.along_z(facing, norm, way.at(which, z - 1), way.at(which, z + 1))
+            shade = way.shade(facing, norm, *sides)
+            sums = [total + saved[z, which, 2 + k] * shade for k, total in enumerate(sums)]
+        parts.append(way.colours(*sums, passed[which]))
+    return parts
 
 
 def store_column(out, x, parts):
@@ -174,7 +218,7 @@
             out[x, channel, pl.ds(which, value.shape[0], stride=2), :] = value
 
 
-def widen_kernel(volume, rows):
+def widen_kernel(depth_total, volume, rows, saved, passed):
     cells_x, cells_z, rows_y = volume.shape
     field = Field(rows, rows_y, cells_x * cells_z)
     field.clear_ends()
@@ -184,16 +228,25 @@
         return 0
 
     lax.fori_loop(0, cells_x, column, 0, unroll=2)
-
-
-def widen(volume):
+    for side, x in ((0, 0), (1, cells_x - 1)):
+        march_to_shading(field, cells_z, x * cells_z, depth_total, saved.at[side], passed.at[side])
+
+
+def widen(volume, depth_total):
     cells_x, cells_z, rows_y = volume.shape
     _, rows = Field.shape(rows_y, cells_x * cells_z)
     return pl.pallas_call(
-        widen_kernel,
-        out_shape=jax.ShapeDtypeStruct((rows, LANES), jnp.float32),
+        lambda *refs: widen_kernel(depth_total, *refs),
+        out_shape=tuple(
+            jax.ShapeDtypeStruct(shape, jnp.float32)
+            for shape in (
+                (rows, LANES),
+                (2, cells_z, 2, 5, rows_y // LANES // 2, LANES),
+                (2, 2, rows_y // LANES // 2, LANES),
+            )
+        ),
         in_specs=[VMEM],
-        out_specs=VMEM,
+        out_specs=(VMEM,) * 3,
         compiler_params=pltpu.CompilerParams(vmem_limit_bytes=12 << 20),
         cost_estimate=pl.CostEstimate(flops=10**6, bytes_accessed=10**6, transcendentals=0),
         name="widen",
@@ -238,22 +291,24 @@
     )(rows, depth_a, depth_b)
 
 
-def outer_kernel(depth_total, rows, depth_a, depth_b, tile_a, tile_b, done, kept, given, scratch, ends, edge):
-    cells_x, rows_y = depth_a.shape
-    cells_z = tile_a.shape[0]
+def outer_kernel(
+    depth_total, rows, depth_a, depth_b, tile_a, tile_b, done, saved, passed, kept, given, scratch, ends, edge
+):
+    cells_z, rows_y = tile_a.shape
+    cells_x = done.shape[0] + 2
     odd_tile = parity("tile")
     field = Field(rows, rows_y, cells_x * cells_z)
     layers = put_layers(scratch, rows_y, depth_a, depth_b)
     halo = Field(ends, rows_y, 2 * cells_z)
     halo.put((1 - odd_tile) * cells_z, tile_a[...].astype(jnp.float32))
     halo.put(odd_tile * cells_z, tile_b[...].astype(jnp.float32) * inside("tile"))
-    final = (cells_x - 1) * cells_z
-    for side, at, left, right in (
-        (0, 0, (halo, 0), (field, cells_z)),
-        (1, final, (field, final - cells_z), (halo, cells_z)),
+    for side, left, right in (
+        (0, (halo, 0), (field, cells_z)),
+        (1, (field, (cells_x - 2) * cells_z), (halo, cells_z)),
     ):
         x = side * (cells_x - 1)
-        parts = march(field, cells_z, at, left, right, (layers, x), (layers, cells_x + x), depth_total)
+        sides = left, right, (layers, x), (layers, cells_x + x)
+        parts = march_shading(field, cells_z, x * cells_z, *sides, saved.at[side], passed.at[side], depth_total)
         store_column(edge, side, parts)
     upper = parity("depth")
     pieces = cells_x // lax.axis_size("depth")
@@ -270,14 +325,14 @@
                 target[i] = done[x - 1]
 
 
-def outer(rows, depth_a, depth_b, tile_a, tile_b, done, depth_total):
-    cells_x, rows_y = depth_a.shape
-    cells_z = tile_a.shape[0]
+def outer(rows, depth_a, depth_b, tile_a, tile_b, done, saved, passed, depth_total):
+    cells_z, rows_y = tile_a.shape
+    cells_x = done.shape[0] + 2
     half = jax.ShapeDtypeStruct((cells_x // 2, 4, rows_y // LANES, LANES), jnp.float32)
     return pl.pallas_call(
         lambda *refs: outer_kernel(depth_total, *refs),
         out_shape=(half, half),
-        in_specs=[VMEM] * 6,
+        in_specs=[VMEM] * 8,
         out_specs=(VMEM, VMEM),
         scratch_shapes=[
             pltpu.VMEM((Field.shape(rows_y, 2 * cells_x)[1], LANES), jnp.float32),
@@ -287,7 +342,7 @@
         compiler_params=pltpu.CompilerParams(vmem_limit_bytes=12 << 20),
         cost_estimate=pl.CostEstimate(flops=10**7, bytes_accessed=10**6, transcendentals=0),
         name="outer",
-    )(rows, depth_a, depth_b, tile_a, tile_b, done)
+    )(rows, depth_a, depth_b, tile_a, tile_b, done, saved, passed)
 
 
 def over(own, other, in_front):
@@ -370,9 +425,9 @@
     depth_b = exchange(depth_b, "depth", 1)
     depth_a = exchange(depth_a, "depth", 0)
     tile_a = exchange(tile_a, "tile", 0)
-    rows = widen(volume)
+    rows, saved, passed = widen(volume, depth_total)
     done = inner(rows, depth_a, depth_b, volume.shape[1], depth_total)
-    kept, given = outer(rows, depth_a, depth_b, tile_a, tile_b, done, depth_total)
+    kept, given = outer(rows, depth_a, depth_b, tile_a, tile_b, done, saved, passed, depth_total)
     for section in range(levels):
         other = lax.ppermute(given, "depth", [(i, i ^ 1 << section) for i in range(depth_count)])
         if section < levels - 1:

time: 21.7 us -> 21.5 us (level)
  waiting for transfers between devices: 6.97 us -> 6.48 us
  Pallas kernels: 8.1 us -> 8.39 us
    pallas_call x1, Pallas kernels: 0.32 us -> 0.81 us  [widen(): pl.pallas_call(lambda *refs: widen_kernel(depth_total, *refs), out_shape=...]
    ppermute x4, waiting for transfers between devices: 2.77 us -> 2.28 us  [exchange(): return lax.ppermute(x, ('tile', 'depth'), found)]
    pallas_call x1, Pallas kernels: 0.78 us -> 0.39 us  [outer(): pl.pallas_call(lambda *refs: outer_kernel(depth_total, *refs), out_shape=...]
  transfers between devices with their start and end apart: 6 -> 6, of which waited for: 3 -> 3; matrix products, arithmetic and copies ran while one was open for 0% -> 0% of each run, Pallas kernels for 24% -> 27%
where the time goes in v1:
time: 21.5 us; the launch traced here: 21.3 us
  Pallas kernels  8.39 us (39%)
  waiting for transfers between devices  6.48 us (30%)
  starting transfers between devices  6.4 us (30%)
    pallas_call x1, Pallas kernels, inner(): pl.pallas_call(lambda *refs: inner_kernel(cells_z, depth_total, *refs), o...  5.03 us
    ppermute x4, starting transfers between devices, exchange(): return lax.ppermute(x, ('tile', 'depth'), found)  4.67 us
    ppermute x2, waiting for transfers between devices, shards(): lax.ppermute(given, 'depth', [(i, i ^ 1 << section) for i in range(depth_...  4.19 us
    ppermute x4, waiting for transfers between devices, exchange(): return lax.ppermute(x, ('tile', 'depth'), found)  2.28 us
    ppermute x2, starting transfers between devices, shards(): lax.ppermute(given, 'depth', [(i, i ^ 1 << section) for i in range(depth_...  1.73 us
    pallas_call x1, Pallas kernels, faces(): pl.pallas_call(faces_kernel, out_shape=(column, column, layer, layer), in...  1.32 us
    pallas_call x1, Pallas kernels, widen(): pl.pallas_call(lambda *refs: widen_kernel(depth_total, *refs), out_shape=...  0.81 us
    pallas_call x1, Pallas kernels, finish(): pl.pallas_call(lambda section_kept, section_other, image: finish_kernel(s...  0.76 us
  transfers between devices with their start and end apart: 6, of which 3 were waited for; matrix products, arithmetic and copies ran while one was open for 0% of the time, Pallas kernels for 27%

profile of v1, /device:TPU:0, one launch (start us, length us, event | category | flops | bytes accessed | tf_op | source)
XLA Modules:
  0.0 21.3 jit_solution(14614312381799801135)
XLA Ops:
  0.0 0.0 copy-start
  0.0 1.3 %faces.1 = (bf16[32,2048]{1,0:T(8,128)(2,1)S(1)}, bf16[32,2048]{1,0:T(8,128)(2,1)S(1)}, bf16[16,2048]{1,0:T(8,128)(2,1)S(1)}, bf16[16,2048]{1,0:T(8,128)(2,1)S(1)}) custom-call(bf16[16,32,2048]{2,1,0:T(8,128)(2,1)} %volume.1), custom_call_target="tpu_custom_call" | custom-call | flops 10000000000 | bytes 1000000 | tf_op jit(solution)/shard_map/faces/pallas_call | solution.py:82
  1.3 3.1 %collective-permute-start.2 = (bf16[32,2048]{1,0:T(8,128)(2,1)S(1)}, bf16[32,2048]{1,0:T(8,128)(2,1)S(1)}, u32[]{:S(2)}, u32[]{:S(2)}) collective-permute-start(bf16[32,2048]{1,0:T(8,128)(2,1)S(1)} %get-tuple-element.19), channel_id=1, source_target_pairs={{0,4},{1,5},{2,6},{3,7},{4,0},{5,1},{6,2},{7,3},{8,12},{9,13},{10,... | collective-permute-start | bytes 393224 | tf_op jit(solution)/shard_map/ppermute | solution.py:42
  4.4 0.0 collective-permute-start.3
  4.4 0.5 %collective-permute-start = (bf16[16,2048]{1,0:T(8,128)(2,1)S(1)}, bf16[16,2048]{1,0:T(8,128)(2,1)S(1)}, u32[]{:S(2)}, u32[]{:S(2)}) collective-permute-start(bf16[16,2048]{1,0:T(8,128)(2,1)S(1)} %get-tuple-element.17), channel_id=1, source_target_pairs={{0,1},{1,0},{2,3},{3,2},{4,5},{5,4},{6,7},{7,6},{8,9},{9,8},{10,11... | collective-permute-start | bytes 196616 | tf_op jit(solution)/shard_map/ppermute | solution.py:42
  4.9 1.1 %collective-permute-start.1 = (bf16[16,2048]{1,0:T(8,128)(2,1)S(1)}, bf16[16,2048]{1,0:T(8,128)(2,1)S(1)}, u32[]{:S(2)}, u32[]{:S(2)}) collective-permute-start(bf16[16,2048]{1,0:T(8,128)(2,1)S(1)} %get-tuple-element.18), channel_id=1, source_target_pairs={{0,3},{1,2},{2,1},{3,0},{4,7},{5,6},{6,5},{7,4},{8,11},{9,10},{10,... | collective-permute-start | bytes 196616 | tf_op jit(solution)/shard_map/ppermute | solution.py:42
  6.0 0.0 copy-done
  6.0 0.8 %widen.1 = (f32[9234,128]{1,0:T(8,128)S(1)}, f32[2,32,2,5,8,128]{5,4,3,2,1,0:T(8,128)S(1)}, f32[2,2,8,128]{3,2,1,0:T(8,128)S(1)}) custom-call(bf16[16,32,2048]{2,1,0:T(8,128)(2,1)S(1)} %copy-done), custom_call_target="tpu_custom_call" | custom-call | flops 1000000 | bytes 1000000 | tf_op jit(solution)/shard_map/widen/pallas_call | solution.py:238
  6.8 0.0 collective-permute-done.refs_1_
  6.8 2.3 %collective-permute-done.1.refs_2_ = bf16[16,2048]{1,0:T(8,128)(2,1)S(1)} collective-permute-done((bf16[16,2048]{1,0:T(8,128)(2,1)S(1)}, bf16[16,2048]{1,0:T(8,128)(2,1)S(1)}, u32[]{:S(2)}, u32[]{:S(2)}) %collective-permute-start.1) | collective-permute-done | bytes 65568 | tf_op jit(solution)/shard_map/ppermute | solution.py:42
  9.1 5.0 %inner.1.refs_5_ = f32[14,4,16,128]{3,2,1,0:T(8,128)S(1)} custom-call(f32[9234,128]{1,0:T(8,128)S(1)} %get-tuple-element.16.refs_0_, bf16[16,2048]{1,0:T(8,128)(2,1)S(1)} %collective-permute-done.refs_1_, bf16[16,2048]{1,0:T(8,128)(2,1)S(1)} %collective-permute-done.1.refs_2_), custom_call_target="tpu_custom_call" | custom-call | flops 100000000 | bytes 10000000 | tf_op jit(solution)/shard_map/inner/pallas_call | solution.py:282
  14.1 0.0 collective-permute-done.2.refs_3_
  14.2 0.0 collective-permute-done.3.refs_4_
  14.2 0.4 %outer.1 = (f32[8,4,16,128]{3,2,1,0:T(8,128)S(1)}, f32[8,4,16,128]{3,2,1,0:T(8,128)S(1)}) custom-call(f32[9234,128]{1,0:T(8,128)S(1)} %get-tuple-element.16.refs_0_, bf16[16,2048]{1,0:T(8,128)(2,1)S(1)} %collective-permute-done.refs_1_, bf16[16,2048]{1,0:T(8,128)(2,1)S(1)} %collective-permute-done.1.refs_2_, ...), custom_call_target="tpu_custom_call" | custom-call | flops 10000000 | bytes 1000000 | tf_op jit(solution)/shard_map/outer/pallas_call | solution.py:332
  14.6 0.2 collective-permute-start.4
  14.7 1.4 %collective-permute-done.4.refs_1_ = f32[8,4,16,128]{3,2,1,0:T(8,128)S(1)} collective-permute-done((f32[8,4,16,128]{3,2,1,0:T(8,128)S(1)}, f32[8,4,16,128]{3,2,1,0:T(8,128)S(1)}, u32[]{:S(2)}, u32[]{:S(2)}) %collective-permute-start.4) | collective-permute-done | bytes 262176 | tf_op jit(solution)/shard_map/ppermute | solution.py:432
  16.2 0.1 merge.1
  16.2 1.6 %collective-permute-start.5 = (bf16[4,4,16,128]{3,2,1,0:T(8,128)(2,1)S(1)}, bf16[4,4,16,128]{3,2,1,0:T(8,128)(2,1)S(1)}, u32[]{:S(2)}, u32[]{:S(2)}) collective-permute-start(bf16[4,4,16,128]{3,2,1,0:T(8,128)(2,1)S(1)} %get-tuple-element.26), channel_id=1, source_target_pairs={{0,2},{1,3},{2,0},{3,1},{4,6},{5,7},{6,4},{7,5},{8,10},{9,11},{10,... | collective-permute-start | bytes 196616 | tf_op jit(solution)/shard_map/ppermute | solution.py:432
  17.8 2.8 %collective-permute-done.5.section_other = bf16[4,4,16,128]{3,2,1,0:T(8,128)(2,1)S(1)} collective-permute-done((bf16[4,4,16,128]{3,2,1,0:T(8,128)(2,1)S(1)}, bf16[4,4,16,128]{3,2,1,0:T(8,128)(2,1)S(1)}, u32[]{:S(2)}, u32[]{:S(2)}) %collective-permute-start.5) | collective-permute-done | bytes 65568 | tf_op jit(solution)/shard_map/ppermute | solution.py:432
  20.6 0.8 %finish.1 = f32[4,4,2048]{2,1,0:T(4,128)} custom-call(f32[4,4,16,128]{3,2,1,0:T(8,128)S(1)} %get-tuple-element.25.section_kept, bf16[4,4,16,128]{3,2,1,0:T(8,128)(2,1)S(1)} %collective-permute-done.5.section_other), custom_call_target="tpu_custom_call" | custom-call | tf_op jit(solution)/shard_map/finish/pallas_call | solution.py:408
Async XLA Ops:
  0.0 6.0 %copy-start = (bf16[16,32,2048]{2,1,0:T(8,128)(2,1)S(1)}, bf16[16,32,2048]{2,1,0:T(8,128)(2,1)}, u32[]{:S(2)}) copy-start(bf16[16,32,2048]{2,1,0:T(8,128)(2,1)} %volume.1) | copy-start | bytes 6291460
  1.3 12.8 %collective-permute-start.2 = (bf16[32,2048]{1,0:T(8,128)(2,1)S(1)}, bf16[32,2048]{1,0:T(8,128)(2,1)S(1)}, u32[]{:S(2)}, u32[]{:S(2)}) collective-permute-start(bf16[32,2048]{1,0:T(8,128)(2,1)S(1)} %get-tuple-element.19), channel_id=1, source_target_pairs={{0,4},{1,5},{2,6},{3,7},{4,0},{5,1},{6,2},{7,3},{8,12},{9,13},{10,... | collective-permute-start | bytes 393224 | tf_op jit(solution)/shard_map/ppermute | solution.py:42
  4.4 9.8 %collective-permute-start.3 = (bf16[32,2048]{1,0:T(8,128)(2,1)S(1)}, bf16[32,2048]{1,0:T(8,128)(2,1)S(1)}, u32[]{:S(2)}, u32[]{:S(2)}) collective-permute-start(bf16[32,2048]{1,0:T(8,128)(2,1)S(1)} %get-tuple-element.20), channel_id=1, source_target_pairs={{0,1},{1,0},{2,3},{3,2},{4,8},{5,9},{6,10},{7,11},{8,4},{9,5},{10,... | collective-permute-start | bytes 393224 | tf_op jit(solution)/shard_map/ppermute | solution.py:42
  4.4 2.4 %collective-permute-start = (bf16[16,2048]{1,0:T(8,128)(2,1)S(1)}, bf16[16,2048]{1,0:T(8,128)(2,1)S(1)}, u32[]{:S(2)}, u32[]{:S(2)}) collective-permute-start(bf16[16,2048]{1,0:T(8,128)(2,1)S(1)} %get-tuple-element.17), channel_id=1, source_target_pairs={{0,1},{1,0},{2,3},{3,2},{4,5},{5,4},{6,7},{7,6},{8,9},{9,8},{10,11... | collective-permute-start | bytes 196616 | tf_op jit(solution)/shard_map/ppermute | solution.py:42
  4.9 4.2 %collective-permute-start.1 = (bf16[16,2048]{1,0:T(8,128)(2,1)S(1)}, bf16[16,2048]{1,0:T(8,128)(2,1)S(1)}, u32[]{:S(2)}, u32[]{:S(2)}) collective-permute-start(bf16[16,2048]{1,0:T(8,128)(2,1)S(1)} %get-tuple-element.18), channel_id=1, source_target_pairs={{0,3},{1,2},{2,1},{3,0},{4,7},{5,6},{6,5},{7,4},{8,11},{9,10},{10,... | collective-permute-start | bytes 196616 | tf_op jit(solution)/shard_map/ppermute | solution.py:42
  14.6 1.6 %collective-permute-start.4 = (f32[8,4,16,128]{3,2,1,0:T(8,128)S(1)}, f32[8,4,16,128]{3,2,1,0:T(8,128)S(1)}, u32[]{:S(2)}, u32[]{:S(2)}) collective-permute-start(f32[8,4,16,128]{3,2,1,0:T(8,128)S(1)} %get-tuple-element.24), channel_id=1, source_target_pairs={{0,1},{1,0},{2,3},{3,2},{4,5},{5,4},{6,7},{7,6},{8,9},{9,8},{10,11... | collective-permute-start | bytes 786440 | tf_op jit(solution)/shard_map/ppermute | solution.py:432
  16.2 4.3 %collective-permute-start.5 = (bf16[4,4,16,128]{3,2,1,0:T(8,128)(2,1)S(1)}, bf16[4,4,16,128]{3,2,1,0:T(8,128)(2,1)S(1)}, u32[]{:S(2)}, u32[]{:S(2)}) collective-permute-start(bf16[4,4,16,128]{3,2,1,0:T(8,128)(2,1)S(1)} %get-tuple-element.26), channel_id=1, source_target_pairs={{0,2},{1,3},{2,0},{3,1},{4,6},{5,7},{6,4},{7,5},{8,10},{9,11},{10,... | collective-permute-start | bytes 196616 | tf_op jit(solution)/shard_map/ppermute | solution.py:432
